TPU v7x, 32 devices: a whole 2x2x4 slice. The times are simulated.
32 devices in a mesh: members: 4 (over y, core), space: 8 (over z, x).
Axes of the slice: x: 2, y: 2, z: 4, core: 2. Of those that a mesh axis runs over, the one named last changes fastest.
Arguments:
- ensemble: float32 [3, 512, 64, 256], P(None, 'members', 'space'), may hold values from -6 to 6
- obs_cells: int32 [8, 4, 128], P('space', 'members'), may hold values from 0 to 1535
- obs_values: float32 [8, 4, 128], P('space', 'members'), may hold values from -6 to 6
- obs_var: float32 [8, 4, 128], P('space', 'members'), may hold values from 0.25 to 4
- obs_noise: float32 [512, 8, 4, 128], P(None, 'space', 'members'), may hold values from -6 to 6
- assign: int32 [512], replicated, may hold values from 0 to 511, each once
Outputs:
- analysis: float32 [3, 512, 64, 256], P(None, 'members', 'space')
Inputs may be any that keep to these rules, and one draw needn't show every extreme that they name: assign holds every member once. obs_cells[r, c, k] = field * 8 * 64 + row * 64 + column within tile (r, c); repeats are possible.
All inputs are finite; a program needn't handle non-finite values.
Results may differ from a plain program's by a relative error of at most 0.0003.
Values sent between devices are 32-bit elements; how exact they have to be, the bound alone decides.
A program may use at most 64 MiB of HBM per device.

v0:
```python
import jax
import jax.numpy as jnp
from jax import lax
from jax.sharding import PartitionSpec as P

TILE_W = 64
STEPS = 4


tstep = 0.1
gravity = 1.0
depth = 1.0
coriolis = 0.25
viscosity = 0.5


def extended(cells, sides, width):
    for axis, dim in sides:
        count = lax.axis_size(axis)
        head = lax.slice_in_dim(cells, 0, width, axis=dim)
        tail = lax.slice_in_dim(cells, cells.shape[dim] - width, cells.shape[dim], axis=dim)
        cells = jnp.concatenate(
            [
                lax.ppermute(tail, axis, [(i, (i + 1) % count) for i in range(count)]),
                cells,
                lax.ppermute(head, axis, [((i + 1) % count, i) for i in range(count)]),
            ],
            axis=dim,
        )
    return cells


def centred_x(field):
    return 0.5 * (jnp.roll(field, -1, axis=2) - jnp.roll(field, 1, axis=2))


def height_update(state):
    eta, east, north = (state[0], state[1], state[2])
    column = depth + eta
    flux_x = centred_x(column * east)[:, 1:-1]
    carried = column * north
    flux_y = 0.5 * (carried[:, 2:] - carried[:, :-2])
    return eta[:, 1:-1] - tstep * (flux_x + flux_y)


def momentum_update(eta, east, north):

    def advance(field, extra):
        inner = field[:, 1:-1]
        grad_x = centred_x(field)[:, 1:-1]
        grad_y = 0.5 * (field[:, 2:] - field[:, :-2])
        spread = (
            jnp.roll(field, -1, axis=2)[:, 1:-1]
            + jnp.roll(field, 1, axis=2)[:, 1:-1]
            + field[:, 2:]
            + field[:, :-2]
            - 4.0 * inner
        )
        return inner + tstep * (
            -east[:, 1:-1] * grad_x - north[:, 1:-1] * grad_y + extra + viscosity * spread
        )

    slope_x = centred_x(eta)[:, 1:-1]
    slope_y = 0.5 * (eta[:, 2:] - eta[:, :-2])
    new_east = advance(east, coriolis * north[:, 1:-1] - gravity * slope_x)
    new_north = advance(north, -coriolis * east[:, 1:-1] - gravity * slope_y)
    return (new_east, new_north)


def thin_pad(state):
    return extended(state, (("space", 2),), 1)


def analyse_tile(tile, near):
    count = tile.shape[1]
    spread_all = jnp.transpose(near[:, :, 0], (2, 0, 1, 3)).reshape(count, -1)
    misfit_all = jnp.transpose(near[:, :, 1], (2, 0, 1, 3)).reshape(count, -1)
    gram = jnp.dot(spread_all, spread_all.T, precision=lax.Precision.HIGHEST) / (
        count - 1
    ) + jnp.eye(count, dtype=jnp.float32)
    factor = jnp.linalg.cholesky(gram)
    reduced = jax.scipy.linalg.cho_solve((factor, True), spread_all)
    mixing = jnp.dot(misfit_all, reduced.T, precision=lax.Precision.HIGHEST) / (count - 1)
    anomaly = tile - jnp.mean(tile, axis=1, keepdims=True)
    return tile + jnp.einsum("ij,fjc->fic", mixing, anomaly, precision=lax.Precision.HIGHEST)


def local(ensemble, obs_cells, obs_values, obs_var, obs_noise, assign):
    state = ensemble
    for step in range(STEPS):
        eta_new = height_update(thin_pad(state))
        padded = thin_pad(jnp.stack([eta_new, state[1], state[2]]))
        east, north = momentum_update(padded[0], padded[1], padded[2])
        state = jnp.stack([eta_new, east, north])
    width = TILE_W
    tiles = lax.all_to_all(state, "members", split_axis=3, concat_axis=1, tiled=True)
    count = tiles.shape[1]
    rows_here = tiles.shape[2]
    tile = tiles.reshape(3, count, rows_here * width)
    tile_cells = rows_here * width
    cells = obs_cells.reshape(-1)
    field_of = cells // tile_cells
    cell_of = cells % tile_cells
    shape = (3, tile_cells, cells.shape[0])
    pick = (
        (lax.broadcasted_iota(jnp.int32, shape, 0) == field_of[None, None, :])
        & (lax.broadcasted_iota(jnp.int32, shape, 1) == cell_of[None, None, :])
    ).astype(jnp.float32)
    observed = jnp.einsum("fmc,fco->mo", tile, pick, precision=lax.Precision.HIGHEST)
    scale = 1.0 / jnp.sqrt(obs_var.reshape(-1))
    mean_obs = jnp.mean(observed, axis=0, keepdims=True)
    spread = (observed - mean_obs) * scale
    noise = jnp.take(obs_noise.reshape(count, -1), assign, axis=0)
    misfit = (obs_values.reshape(-1)[None, :] - observed) * scale + noise
    packed = jnp.stack([spread, misfit])[None, None]
    near = extended(packed, (("members", 1), ("space", 0)), 1)
    updated = analyse_tile(tile, near).reshape(3, count, rows_here, width)
    return lax.all_to_all(updated, "members", split_axis=1, concat_axis=3, tiled=True)


def solution(mesh):
    in_specs = (
        P(None, "members", "space", None),
        P("space", "members", None),
        P("space", "members", None),
        P("space", "members", None),
        P(None, "space", "members", None),
        P(),
    )
    out_specs = P(None, "members", "space", None)
    return jax.shard_map(local, mesh=mesh, in_specs=in_specs, out_specs=out_specs, check_vma=False)
```

profile of v0, /device:TPU:0, one launch (start us, length us, event | category | flops | bytes accessed | tf_op | source)
XLA Modules:
  0.0 610.9 jit_solution(4791062386174462947)
XLA Ops:
  0.0 2.6 copy.52
  3.1 3.0 collective-permute-start
  6.1 3.1 collective-permute-start.1
  9.4 13.6 %collective-permute-done = f32[3,128,1,256]{1,2,3,0:T(1,128)S(1)} collective-permute-done((f32[3,128,1,256]{1,2,3,0:T(1,128)S(1)}, f32[3,128,1,256]{1,2,3,0:T(1,128)S(1)}, u32[]{:S(2)}, u32[]{:S(2)}) %collective-permute-start) | collective-permute-done | bytes 393248 | tf_op jit(solution)/shard_map/ppermute | solution.py:24
  22.9 2.2 collective-permute-done.1
  28.7 4.4 collective-permute-start.3
  33.1 11.5 %collective-permute-done.2 = f32[3,128,1,256]{1,2,3,0:T(1,128)S(1)} collective-permute-done((f32[3,128,1,256]{1,2,3,0:T(1,128)S(1)}, f32[3,128,1,256]{1,2,3,0:T(1,128)S(1)}, u32[]{:S(2)}, u32[]{:S(2)}) %collective-permute-start.2) | collective-permute-done | bytes 393248 | tf_op jit(solution)/shard_map/ppermute | solution.py:24
  44.6 3.9 collective-permute-done.3
  55.4 5.0 collective-permute-start.5
  60.4 11.6 %collective-permute-done.4 = f32[3,128,1,256]{1,2,3,0:T(1,128)S(1)} collective-permute-done((f32[3,128,1,256]{1,2,3,0:T(1,128)S(1)}, f32[3,128,1,256]{1,2,3,0:T(1,128)S(1)}, u32[]{:S(2)}, u32[]{:S(2)}) %collective-permute-start.4) | collective-permute-done | bytes 393248 | tf_op jit(solution)/shard_map/ppermute | solution.py:24
  72.0 4.1 collective-permute-done.5
  79.9 4.7 collective-permute-start.7
  84.6 11.7 %collective-permute-done.6 = f32[3,128,1,256]{1,2,3,0:T(1,128)S(1)} collective-permute-done((f32[3,128,1,256]{1,2,3,0:T(1,128)S(1)}, f32[3,128,1,256]{1,2,3,0:T(1,128)S(1)}, u32[]{:S(2)}, u32[]{:S(2)}) %collective-permute-start.6) | collective-permute-done | bytes 393248 | tf_op jit(solution)/shard_map/ppermute | solution.py:24
  96.3 3.7 collective-permute-done.7
  107.2 4.7 collective-permute-start.9
  111.9 11.7 %collective-permute-done.8 = f32[3,128,1,256]{1,2,3,0:T(1,128)S(1)} collective-permute-done((f32[3,128,1,256]{1,2,3,0:T(1,128)S(1)}, f32[3,128,1,256]{1,2,3,0:T(1,128)S(1)}, u32[]{:S(2)}, u32[]{:S(2)}) %collective-permute-start.8) | collective-permute-done | bytes 393248 | tf_op jit(solution)/shard_map/ppermute | solution.py:24
  123.6 2.3 collective-permute-done.9
  130.0 5.0 collective-permute-start.11
  135.0 10.5 %collective-permute-done.10 = f32[3,128,1,256]{1,2,3,0:T(1,128)S(1)} collective-permute-done((f32[3,128,1,256]{1,2,3,0:T(1,128)S(1)}, f32[3,128,1,256]{1,2,3,0:T(1,128)S(1)}, u32[]{:S(2)}, u32[]{:S(2)}) %collective-permute-start.10) | collective-permute-done | bytes 393248 | tf_op jit(solution)/shard_map/ppermute | solution.py:24
  145.5 4.6 collective-permute-done.11
  157.3 4.7 collective-permute-start.13
  162.0 12.4 %collective-permute-done.12 = f32[3,128,1,256]{1,2,3,0:T(1,128)S(1)} collective-permute-done((f32[3,128,1,256]{1,2,3,0:T(1,128)S(1)}, f32[3,128,1,256]{1,2,3,0:T(1,128)S(1)}, u32[]{:S(2)}, u32[]{:S(2)}) %collective-permute-start.12) | collective-permute-done | bytes 393248 | tf_op jit(solution)/shard_map/ppermute | solution.py:24
  174.5 2.7 collective-permute-done.13
  181.1 4.9 collective-permute-start.15
  186.0 11.5 %collective-permute-done.14 = f32[3,128,1,256]{1,2,3,0:T(1,128)S(1)} collective-permute-done((f32[3,128,1,256]{1,2,3,0:T(1,128)S(1)}, f32[3,128,1,256]{1,2,3,0:T(1,128)S(1)}, u32[]{:S(2)}, u32[]{:S(2)}) %collective-permute-start.14) | collective-permute-done | bytes 393248 | tf_op jit(solution)/shard_map/ppermute | solution.py:24
  197.5 4.1 collective-permute-done.15
  209.8 3.8 all-to-all-start
  217.2 33.3 %all-to-all-done = f32[3,128,8,256]{1,2,0,3:T(8,128)S(1)} async-done(((f32[3,128,8,256]{1,2,0,3:T(8,128)}), f32[3,128,8,256]{1,2,0,3:T(8,128)S(1)}, u32[]{:S(2)}, u32[]{:S(2)}) %all-to-all-start) | async-done | bytes 3145760 | tf_op jit(solution)/shard_map/all_to_all | solution.py:96
  250.5 3.7 copy.59
  254.2 5.0 reshape.97
  259.2 3.4 fusion.313
  263.4 11.2 %collective-permute-done.17 = f32[1,1,2,512,128]{3,4,2,1,0:T(8,128)S(1)} collective-permute-done((f32[1,1,2,512,128]{3,4,2,1,0:T(8,128)S(1)}, f32[1,1,2,512,128]{3,4,2,1,0:T(8,128)S(1)}, u32[]{:S(2)}, u32[]{:S(2)}) %collective-permute-start.17) | collective-permute-done | bytes 524320 | tf_op jit(solution)/shard_map/ppermute | solution.py:26
  274.6 2.2 collective-permute-done.16
  280.3 2.2 copy.58
  282.5 2.3 reduce_sum.18
  284.9 63.5 %collective-permute-done.19 = f32[1,3,2,512,128]{3,4,2,1,0:T(8,128)} collective-permute-done((f32[1,3,2,512,128]{3,4,2,1,0:T(8,128)}, f32[1,3,2,512,128]{3,4,2,1,0:T(8,128)}, u32[]{:S(2)}, u32[]{:S(2)}) %collective-permute-start.19) | collective-permute-done | bytes 1572896 | tf_op jit(solution)/shard_map/ppermute | solution.py:26
  348.4 2.3 pad_maximum_fusion.14
  350.8 5.7 convert_add_fusion
  356.4 2.1 slice_bitcast_fusion
  358.6 2.6 copy.65
  363.9 11.7 %cholesky.104 = f32[128,128]{1,0:T(8,128)S(1)} custom-call(f32[128,128]{1,0:T(8,128)S(1)} %cholesky.266), custom_call_target="Cholesky" | custom-call | tf_op jit(solution)/shard_map/jit(cholesky)/cholesky | solution.py:81
  378.2 2.3 copy.67
  381.1 10.2 %custom-call.34 = f32[1,128,128]{1,2,0:T(8,128)S(1)} custom-call(f32[1,128,128]{2,1,0:T(8,128)S(1)} %get-tuple-element.140), custom_call_target="InvertDiagBlocksLowerTriangular" | custom-call | tf_op jit(solution)/shard_map/jit(cholesky)/cholesky | solution.py:81
  391.3 2.1 copy.66
  393.4 2.1 copy.68
  396.2 11.7 %cholesky.217 = f32[128,128]{1,0:T(8,128)S(1)} custom-call(f32[128,128]{1,0:T(8,128)S(1)} %cholesky.270), custom_call_target="Cholesky" | custom-call | tf_op jit(solution)/shard_map/jit(cholesky)/cholesky | solution.py:81
  408.6 9.8 %custom-call.35 = f32[1,128,128]{1,2,0:T(8,128)S(1)} custom-call(f32[1,128,128]{2,1,0:T(8,128)S(1)} %get-tuple-element.137), custom_call_target="InvertDiagBlocksLowerTriangular" | custom-call | tf_op jit(solution)/shard_map/jit(cholesky)/cholesky | solution.py:81
  419.1 11.7 %cholesky.238 = f32[128,128]{1,0:T(8,128)S(1)} custom-call(f32[128,128]{1,0:T(8,128)S(1)} %cholesky.275), custom_call_target="Cholesky" | custom-call | tf_op jit(solution)/shard_map/jit(cholesky)/cholesky | solution.py:81
  431.6 9.9 %custom-call.36 = f32[1,128,128]{1,2,0:T(8,128)S(1)} custom-call(f32[1,128,128]{2,1,0:T(8,128)S(1)} %get-tuple-element.134), custom_call_target="InvertDiagBlocksLowerTriangular" | custom-call | tf_op jit(solution)/shard_map/jit(cholesky)/cholesky | solution.py:81
  442.1 11.7 %cholesky.255 = f32[128,128]{1,0:T(8,128)S(1)} custom-call(f32[128,128]{1,0:T(8,128)S(1)} %convolution_subtract_fusion.8), custom_call_target="Cholesky" | custom-call | tf_op jit(solution)/shard_map/jit(cholesky)/cholesky | solution.py:81
  457.1 10.6 %while.1 = (s32[]{:T(128)}, f32[512,512]{1,0:T(8,128)S(1)}, s32[4,2]{0,1:T(2,128)S(1)}, f32[4,128,128]{2,1,0:T(8,128)}, s32[]{:T(128)}) while((s32[]{:T(128)}, f32[512,512]{1,0:T(8,128)S(1)}, s32[4,2]{0,1:T(2,128)S(1)}, f32[4,128,128]{2,1,0:T(8,128)}, s32[]{:T(128)}) %tuple.90), condition=%wide.while_cond, body=%wide.while_body.sunk | while | flops 2 | bytes 132205 | solution.py:82
  460.4 2.0 bitcast_dynamic-update-slice_fusion.2
  463.1 2.0 bitcast_dynamic-update-slice_fusion.2
  467.7 40.3 %custom-call.37 = f32[4,128,128]{1,2,0:T(8,128)S(1)} custom-call(f32[4,128,128]{2,1,0:T(8,128)} %get-tuple-element.12), custom_call_target="InvertDiagBlocksLowerTriangular" | custom-call | tf_op jit(solution)/shard_map/jit(_cho_solve)/triangular_solve | solution.py:82
  519.1 4.8 fusion.49
  523.9 5.4 bitcast_add_fusion
  529.3 4.2 copy.71
  533.5 7.0 %reshape.132 = f32[4,1,196608]{2,1,0:T(1,128)} reshape(f32[512,3,8,64]{3,2,1,0:T(8,128)} %bitcast.224) | data formatting | bytes 6291456
  540.6 40.7 %all_to_all.33 = f32[4,1,196608]{2,1,0:T(1,128)S(1)} all-to-all(f32[4,1,196608]{2,1,0:T(1,128)} %reshape.132), channel_id=1, replica_groups=mesh['members'=4,'space'=8] {'members'}, dimensions={0} | all-to-all | bytes 6291456 | tf_op jit(solution)/shard_map/all_to_all | solution.py:118
  581.9 10.6 %reduce.25 = f32[4,196608]{1,0:T(4,128)} reduce(f32[4,1,196608]{2,1,0:T(1,128)S(1)} %all_to_all.33, f32[]{:T(128)} %broadcast.379), dimensions={1}, to_apply=%all_to_all.27.reduce_sub_computation | reduce | bytes 6291460 | tf_op jit(solution)/shard_map/all_to_all | solution.py:118
  592.5 7.4 %reshape.133 = f32[512,3,8,64]{3,2,1,0:T(8,128)} reshape(f32[4,196608]{1,0:T(4,128)} %reduce.25) | data formatting | bytes 6291456
  599.9 6.1 %copy.84 = f32[3,4,128,8,64]{2,1,4,3,0:T(4,128)} copy(f32[3,4,128,8,64]{4,3,0,2,1:T(8,128)} %bitcast.225) | data formatting | bytes 6291456 | tf_op jit(solution)/shard_map/all_to_all | solution.py:118
  606.0 2.3 copy.73
  608.4 2.4 copy.74
  (192 shorter events, 80.8 us)
Async XLA Ops:
  0.0 213.7 %copy-start = (f32[512,1,1,128]{3,2,1,0:T(1,128)S(1)}, f32[512,1,1,128]{3,2,1,0:T(1,128)}, u32[]{:S(2)}) copy-start(f32[512,1,1,128]{3,2,1,0:T(1,128)} %param.10) | copy-start | bytes 786436
  3.1 19.8 %collective-permute-start = (f32[3,128,1,256]{1,2,3,0:T(1,128)S(1)}, f32[3,128,1,256]{1,2,3,0:T(1,128)S(1)}, u32[]{:S(2)}, u32[]{:S(2)}) collective-permute-start(f32[3,128,1,256]{1,2,3,0:T(1,128)S(1)} %get-tuple-element.59), channel_id=1, source_target_pairs={{0,1},{1,2},{2,3},{3,4},{4,5},{5,6},{6,7},{7,0},{8,9},{9,10},{10,1... | collective-permute-start | bytes 1179656 | tf_op jit(solution)/shard_map/ppermute | solution.py:24
  6.1 19.0 %collective-permute-start.1 = (f32[3,128,1,256]{1,2,3,0:T(1,128)S(1)}, f32[3,128,1,256]{1,2,3,0:T(1,128)S(1)}, u32[]{:S(2)}, u32[]{:S(2)}) collective-permute-start(f32[3,128,1,256]{1,2,3,0:T(1,128)S(1)} %get-tuple-element.60), channel_id=1, source_target_pairs={{1,0},{2,1},{3,2},{4,3},{5,4},{6,5},{7,6},{0,7},{9,8},{10,9},{11,1... | collective-permute-start | bytes 1179656 | tf_op jit(solution)/shard_map/ppermute | solution.py:26
  28.4 16.3 %collective-permute-start.2 = (f32[3,128,1,256]{1,2,3,0:T(1,128)S(1)}, f32[3,128,1,256]{1,2,3,0:T(1,128)S(1)}, u32[]{:S(2)}, u32[]{:S(2)}) collective-permute-start(f32[3,128,1,256]{1,2,3,0:T(1,128)S(1)} %get-tuple-element.57), channel_id=1, source_target_pairs={{0,1},{1,2},{2,3},{3,4},{4,5},{5,6},{6,7},{7,0},{8,9},{9,10},{10,1... | collective-permute-start | bytes 1179656 | tf_op jit(solution)/shard_map/ppermute | solution.py:24
  28.7 19.9 %collective-permute-start.3 = (f32[3,128,1,256]{1,2,3,0:T(1,128)S(1)}, f32[3,128,1,256]{1,2,3,0:T(1,128)S(1)}, u32[]{:S(2)}, u32[]{:S(2)}) collective-permute-start(f32[3,128,1,256]{1,2,3,0:T(1,128)S(1)} %get-tuple-element.58), channel_id=1, source_target_pairs={{1,0},{2,1},{3,2},{4,3},{5,4},{6,5},{7,6},{0,7},{9,8},{10,9},{11,1... | collective-permute-start | bytes 1179656 | tf_op jit(solution)/shard_map/ppermute | solution.py:26
  55.3 16.6 %collective-permute-start.4 = (f32[3,128,1,256]{1,2,3,0:T(1,128)S(1)}, f32[3,128,1,256]{1,2,3,0:T(1,128)S(1)}, u32[]{:S(2)}, u32[]{:S(2)}) collective-permute-start(f32[3,128,1,256]{1,2,3,0:T(1,128)S(1)} %get-tuple-element.55), channel_id=1, source_target_pairs={{0,1},{1,2},{2,3},{3,4},{4,5},{5,6},{6,7},{7,0},{8,9},{9,10},{10,1... | collective-permute-start | bytes 1179656 | tf_op jit(solution)/shard_map/ppermute | solution.py:24
  55.4 20.6 %collective-permute-start.5 = (f32[3,128,1,256]{1,2,3,0:T(1,128)S(1)}, f32[3,128,1,256]{1,2,3,0:T(1,128)S(1)}, u32[]{:S(2)}, u32[]{:S(2)}) collective-permute-start(f32[3,128,1,256]{1,2,3,0:T(1,128)S(1)} %get-tuple-element.56), channel_id=1, source_target_pairs={{1,0},{2,1},{3,2},{4,3},{5,4},{6,5},{7,6},{0,7},{9,8},{10,9},{11,1... | collective-permute-start | bytes 1179656 | tf_op jit(solution)/shard_map/ppermute | solution.py:26
  79.9 16.5 %collective-permute-start.6 = (f32[3,128,1,256]{1,2,3,0:T(1,128)S(1)}, f32[3,128,1,256]{1,2,3,0:T(1,128)S(1)}, u32[]{:S(2)}, u32[]{:S(2)}) collective-permute-start(f32[3,128,1,256]{1,2,3,0:T(1,128)S(1)} %get-tuple-element.53), channel_id=1, source_target_pairs={{0,1},{1,2},{2,3},{3,4},{4,5},{5,6},{6,7},{7,0},{8,9},{9,10},{10,1... | collective-permute-start | bytes 1179656 | tf_op jit(solution)/shard_map/ppermute | solution.py:24
  79.9 20.1 %collective-permute-start.7 = (f32[3,128,1,256]{1,2,3,0:T(1,128)S(1)}, f32[3,128,1,256]{1,2,3,0:T(1,128)S(1)}, u32[]{:S(2)}, u32[]{:S(2)}) collective-permute-start(f32[3,128,1,256]{1,2,3,0:T(1,128)S(1)} %get-tuple-element.54), channel_id=1, source_target_pairs={{1,0},{2,1},{3,2},{4,3},{5,4},{6,5},{7,6},{0,7},{9,8},{10,9},{11,1... | collective-permute-start | bytes 1179656 | tf_op jit(solution)/shard_map/ppermute | solution.py:26
  107.1 16.5 %collective-permute-start.8 = (f32[3,128,1,256]{1,2,3,0:T(1,128)S(1)}, f32[3,128,1,256]{1,2,3,0:T(1,128)S(1)}, u32[]{:S(2)}, u32[]{:S(2)}) collective-permute-start(f32[3,128,1,256]{1,2,3,0:T(1,128)S(1)} %get-tuple-element.51), channel_id=1, source_target_pairs={{0,1},{1,2},{2,3},{3,4},{4,5},{5,6},{6,7},{7,0},{8,9},{9,10},{10,1... | collective-permute-start | bytes 1179656 | tf_op jit(solution)/shard_map/ppermute | solution.py:24
  107.2 18.7 %collective-permute-start.9 = (f32[3,128,1,256]{1,2,3,0:T(1,128)S(1)}, f32[3,128,1,256]{1,2,3,0:T(1,128)S(1)}, u32[]{:S(2)}, u32[]{:S(2)}) collective-permute-start(f32[3,128,1,256]{1,2,3,0:T(1,128)S(1)} %get-tuple-element.52), channel_id=1, source_target_pairs={{1,0},{2,1},{3,2},{4,3},{5,4},{6,5},{7,6},{0,7},{9,8},{10,9},{11,1... | collective-permute-start | bytes 1179656 | tf_op jit(solution)/shard_map/ppermute | solution.py:26
  129.7 15.8 %collective-permute-start.10 = (f32[3,128,1,256]{1,2,3,0:T(1,128)S(1)}, f32[3,128,1,256]{1,2,3,0:T(1,128)S(1)}, u32[]{:S(2)}, u32[]{:S(2)}) collective-permute-start(f32[3,128,1,256]{1,2,3,0:T(1,128)S(1)} %get-tuple-element.49), channel_id=1, source_target_pairs={{0,1},{1,2},{2,3},{3,4},{4,5},{5,6},{6,7},{7,0},{8,9},{9,10},{10,1... | collective-permute-start | bytes 1179656 | tf_op jit(solution)/shard_map/ppermute | solution.py:24
  130.0 20.2 %collective-permute-start.11 = (f32[3,128,1,256]{1,2,3,0:T(1,128)S(1)}, f32[3,128,1,256]{1,2,3,0:T(1,128)S(1)}, u32[]{:S(2)}, u32[]{:S(2)}) collective-permute-start(f32[3,128,1,256]{1,2,3,0:T(1,128)S(1)} %get-tuple-element.50), channel_id=1, source_target_pairs={{1,0},{2,1},{3,2},{4,3},{5,4},{6,5},{7,6},{0,7},{9,8},{10,9},{11,1... | collective-permute-start | bytes 1179656 | tf_op jit(solution)/shard_map/ppermute | solution.py:26
  157.3 17.2 %collective-permute-start.12 = (f32[3,128,1,256]{1,2,3,0:T(1,128)S(1)}, f32[3,128,1,256]{1,2,3,0:T(1,128)S(1)}, u32[]{:S(2)}, u32[]{:S(2)}) collective-permute-start(f32[3,128,1,256]{1,2,3,0:T(1,128)S(1)} %get-tuple-element.47), channel_id=1, source_target_pairs={{0,1},{1,2},{2,3},{3,4},{4,5},{5,6},{6,7},{7,0},{8,9},{9,10},{10,1... | collective-permute-start | bytes 1179656 | tf_op jit(solution)/shard_map/ppermute | solution.py:24
  157.3 19.8 %collective-permute-start.13 = (f32[3,128,1,256]{1,2,3,0:T(1,128)S(1)}, f32[3,128,1,256]{1,2,3,0:T(1,128)S(1)}, u32[]{:S(2)}, u32[]{:S(2)}) collective-permute-start(f32[3,128,1,256]{1,2,3,0:T(1,128)S(1)} %get-tuple-element.48), channel_id=1, source_target_pairs={{1,0},{2,1},{3,2},{4,3},{5,4},{6,5},{7,6},{0,7},{9,8},{10,9},{11,1... | collective-permute-start | bytes 1179656 | tf_op jit(solution)/shard_map/ppermute | solution.py:26
  181.0 16.5 %collective-permute-start.14 = (f32[3,128,1,256]{1,2,3,0:T(1,128)S(1)}, f32[3,128,1,256]{1,2,3,0:T(1,128)S(1)}, u32[]{:S(2)}, u32[]{:S(2)}) collective-permute-start(f32[3,128,1,256]{1,2,3,0:T(1,128)S(1)} %get-tuple-element.45), channel_id=1, source_target_pairs={{0,1},{1,2},{2,3},{3,4},{4,5},{5,6},{6,7},{7,0},{8,9},{9,10},{10,1... | collective-permute-start | bytes 1179656 | tf_op jit(solution)/shard_map/ppermute | solution.py:24
  181.1 20.5 %collective-permute-start.15 = (f32[3,128,1,256]{1,2,3,0:T(1,128)S(1)}, f32[3,128,1,256]{1,2,3,0:T(1,128)S(1)}, u32[]{:S(2)}, u32[]{:S(2)}) collective-permute-start(f32[3,128,1,256]{1,2,3,0:T(1,128)S(1)} %get-tuple-element.46), channel_id=1, source_target_pairs={{1,0},{2,1},{3,2},{4,3},{5,4},{6,5},{7,6},{0,7},{9,8},{10,9},{11,1... | collective-permute-start | bytes 1179656 | tf_op jit(solution)/shard_map/ppermute | solution.py:26
  209.8 3.8 copy-start.16
  209.8 40.7 %all-to-all-start = ((f32[3,128,8,256]{1,2,0,3:T(8,128)}), f32[3,128,8,256]{1,2,0,3:T(8,128)S(1)}, u32[]{:S(2)}, u32[]{:S(2)}) async-start(f32[3,128,8,256]{1,2,0,3:T(8,128)} %pad_maximum_fusion.27), calls=%async_computation | async-start | bytes 6291456 | tf_op jit(solution)/shard_map/all_to_all | solution.py:96
  213.6 3.5 copy-start.18
  213.7 3.5 copy-start.19
  259.2 3.4 copy-start.15
  259.2 3.4 copy-start.17
  262.8 14.0 %copy-start.3 = (f32[1,1,2,512,128]{3,4,2,1,0:T(8,128)}, f32[1,1,2,512,128]{3,4,2,1,0:T(8,128)S(1)}, u32[]{:S(2)}) copy-start(f32[1,1,2,512,128]{3,4,2,1,0:T(8,128)S(1)} %maximum_bitcast_fusion) | copy-start | bytes 1572868
  262.8 11.8 %collective-permute-start.17 = (f32[1,1,2,512,128]{3,4,2,1,0:T(8,128)S(1)}, f32[1,1,2,512,128]{3,4,2,1,0:T(8,128)S(1)}, u32[]{:S(2)}, u32[]{:S(2)}) collective-permute-start(f32[1,1,2,512,128]{3,4,2,1,0:T(8,128)S(1)} %maximum_bitcast_fusion), channel_id=1, source_target_pairs={{8,0},{16,8},{24,16},{0,24},{9,1},{17,9},{25,17},{1,25},{10,2},{18... | collective-permute-start | bytes 1572872 | tf_op jit(solution)/shard_map/ppermute | solution.py:26
  262.9 13.9 %collective-permute-start.16 = (f32[1,1,2,512,128]{3,4,2,1,0:T(8,128)S(1)}, f32[1,1,2,512,128]{3,4,2,1,0:T(8,128)S(1)}, u32[]{:S(2)}, u32[]{:S(2)}) collective-permute-start(f32[1,1,2,512,128]{3,4,2,1,0:T(8,128)S(1)} %maximum_bitcast_fusion), channel_id=1, source_target_pairs={{0,8},{8,16},{16,24},{24,0},{1,9},{9,17},{17,25},{25,1},{2,10},{10... | collective-permute-start | bytes 1572872 | tf_op jit(solution)/shard_map/ppermute | solution.py:24
  274.6 3.6 copy-start.11
  276.8 2.8 copy-start.13
  278.2 70.2 %collective-permute-start.19 = (f32[1,3,2,512,128]{3,4,2,1,0:T(8,128)}, f32[1,3,2,512,128]{3,4,2,1,0:T(8,128)}, u32[]{:S(2)}, u32[]{:S(2)}) collective-permute-start(f32[1,3,2,512,128]{3,4,2,1,0:T(8,128)} %pad_maximum_fusion.28), channel_id=1, source_target_pairs={{1,0},{2,1},{3,2},{4,3},{5,4},{6,5},{7,6},{0,7},{9,8},{10,9},{11,1... | collective-permute-start | bytes 4718600 | tf_op jit(solution)/shard_map/ppermute | solution.py:26
  279.6 68.8 %collective-permute-start.18 = (f32[1,3,2,512,128]{3,4,2,1,0:T(8,128)}, f32[1,3,2,512,128]{3,4,2,1,0:T(8,128)}, u32[]{:S(2)}, u32[]{:S(2)}) collective-permute-start(f32[1,3,2,512,128]{3,4,2,1,0:T(8,128)} %pad_maximum_fusion.28), channel_id=1, source_target_pairs={{0,1},{1,2},{2,3},{3,4},{4,5},{5,6},{6,7},{7,0},{8,9},{9,10},{10,1... | collective-permute-start | bytes 4718600 | tf_op jit(solution)/shard_map/ppermute | solution.py:24
  282.5 65.9 %copy-start.4 = (f32[1,1,2,512,128]{3,4,2,1,0:T(8,128)S(1)}, f32[1,1,2,512,128]{3,4,2,1,0:T(8,128)}, u32[]{:S(2)}) copy-start(f32[1,1,2,512,128]{3,4,2,1,0:T(8,128)} %copy-done.3) | copy-start | bytes 1572868
  282.5 65.9 %copy-start.12 = (f32[1,1,2,512,128]{3,4,2,1,0:T(8,128)S(1)}, f32[1,1,2,512,128]{3,4,2,1,0:T(8,128)}, u32[]{:S(2)}) copy-start(f32[1,1,2,512,128]{3,4,2,1,0:T(8,128)} %copy-done.11) | copy-start | bytes 1572868
  282.5 65.9 %copy-start.14 = (f32[1,1,2,512,128]{3,4,2,1,0:T(8,128)S(1)}, f32[1,1,2,512,128]{3,4,2,1,0:T(8,128)}, u32[]{:S(2)}) copy-start(f32[1,1,2,512,128]{3,4,2,1,0:T(8,128)} %copy-done.13) | copy-start | bytes 1572868
  362.9 1.0 copy-start.5
  378.2 17.4 %copy-start.2 = (f32[512,512]{1,0:T(8,128)S(1)}, f32[512,512]{1,0:T(8,128)}, u32[]{:S(2)}) copy-start(f32[512,512]{1,0:T(8,128)} %cholesky.224) | copy-start | bytes 3145732
  378.2 17.4 %copy-start.6 = (f32[512,512]{1,0:T(8,128)S(1)}, f32[512,512]{1,0:T(8,128)}, u32[]{:S(2)}) copy-start(f32[512,512]{1,0:T(8,128)} %copy-done.5) | copy-start | bytes 3145732
  457.1 51.7 %copy-start.8 = (f32[128,1152]{1,0:T(8,128)S(1)}, f32[128,1152]{1,0:T(8,128)}, u32[]{:S(2)}) copy-start(f32[128,1152]{1,0:T(8,128)} %copy.66) | copy-start | bytes 1769476
  508.1 2.1 copy-start.7
  510.1 1.5 copy-start.9
  517.1 2.0 copy-start.10
  519.0 4.8 copy-start.1
where the time goes:
time: 619 us; the launch traced here: 611 us
  waiting for transfers between devices  232 us (37%)
  other arithmetic  173 us (28%)
  local copies, waits for them, and re-layouts  82.7 us (13%)
  starting transfers between devices  46.8 us (8%)
  blocking collectives  40.7 us (7%)
  matrix products  31.9 us (5%)
    ppermute x10, waiting for transfers between devices, extended(): lax.ppermute(head, axis, [((i + 1) % count, i) for i in range(count)])  102 us
    ppermute x10, waiting for transfers between devices, extended(): lax.ppermute(tail, axis, [(i, (i + 1) % count) for i in range(count)])  96.8 us
    another operation x15, other arithmetic, analyse_tile(): factor = jnp.linalg.cholesky(gram)  79.6 us
    all_to_all x1, blocking collectives, local(): lax.all_to_all(updated, 'members', split_axis=1, concat_axis=3, tiled=True)  40.7 us
    another operation x3, other arithmetic, analyse_tile(): reduced = jax.scipy.linalg.cho_solve((factor, True), spread_all)  40.5 us
    ppermute x10, starting transfers between devices, extended(): lax.ppermute(head, axis, [((i + 1) % count, i) for i in range(count)])  38 us
    all_to_all x1, waiting for transfers between devices, local(): lax.all_to_all(state, 'members', split_axis=3, concat_axis=1, tiled=True)  33.3 us
    another operation x15, other arithmetic, local(): state = jnp.stack([eta_new, east, north])  18.8 us
  transfers between devices with their start and end apart: 21, of which 20 were waited for; matrix products, arithmetic and copies ran while one was open for 1% of the time, Pallas kernels for 0%

commit v1 on v0

v1 whole, which is shorter than its diff:
```python
import functools

import jax
import jax.numpy as jnp
from jax import lax
from jax.experimental import pallas as pl
from jax.experimental.pallas import tpu as pltpu
from jax.sharding import PartitionSpec as P

TILE_W = 64
STEPS = 4
BLOCK = 128

tstep = 0.1
gravity = 1.0
depth = 1.0
coriolis = 0.25
viscosity = 0.5

HIGHEST = lax.Precision.HIGHEST


def forecast_kernel(cols, half, x_ref, y_ref):
    parts, _, _, rows, nx = x_ref.shape
    ny = parts * rows
    member = pl.program_id(0)

    def neighbours(f):
        return (
            pltpu.roll(f, nx - 1, 1),
            pltpu.roll(f, 1, 1),
            pltpu.roll(f, ny - 1, 0),
            pltpu.roll(f, 1, 0),
        )

    eta, east, north = (x_ref[:, f, 0].reshape(ny, nx) for f in range(3))
    for _ in range(STEPS):
        column = depth + eta
        flux = column * east
        carried = column * north
        div = 0.5 * (pltpu.roll(flux, nx - 1, 1) - pltpu.roll(flux, 1, 1)) + 0.5 * (
            pltpu.roll(carried, ny - 1, 0) - pltpu.roll(carried, 1, 0)
        )
        eta = eta - tstep * div
        right, left, below, above = neighbours(eta)
        slope_x = 0.5 * (right - left)
        slope_y = 0.5 * (below - above)

        def advance(field, extra):
            right, left, below, above = neighbours(field)
            grad_x = 0.5 * (right - left)
            grad_y = 0.5 * (below - above)
            lap = right + left + below + above - 4.0 * field
            return field + tstep * (
                -east * grad_x - north * grad_y + extra + viscosity * lap
            )

        new_east = advance(east, coriolis * north - gravity * slope_x)
        new_north = advance(north, -coriolis * east - gravity * slope_y)
        east, north = new_east, new_north

    width = nx // cols
    lane = lax.broadcasted_iota(jnp.int32, (rows, 2 * width), 1)
    low = lane < width
    for f, field in enumerate((eta, east, north)):
        for r in range(parts):
            for p in range(cols // 2):
                v = field[r * rows : (r + 1) * rows, 2 * p * width : 2 * (p + 1) * width]
                turned = pltpu.roll(v, half, 0)
                first = jnp.where(low, v, pltpu.roll(turned, width, 1))
                second = jnp.where(low, pltpu.roll(v, width, 1), turned)
                for q in range(half):
                    y_ref[2 * p, r, f, q, pl.ds(member, 1), :] = first[q : q + 1]
                    y_ref[2 * p + 1, r, f, q, pl.ds(member, 1), :] = second[q : q + 1]


def forecast(x, cols):
    parts, fields, members, rows, nx = x.shape
    half = rows // 2
    return pl.pallas_call(
        functools.partial(forecast_kernel, cols, half),
        grid=(members,),
        in_specs=[pl.BlockSpec((parts, fields, 1, rows, nx), lambda j: (0, 0, j, 0, 0))],
        out_specs=pl.BlockSpec(
            (cols, parts, fields, half, members, 2 * nx // cols), lambda j: (0, 0, 0, 0, 0, 0)
        ),
        out_shape=jax.ShapeDtypeStruct(
            (cols, parts, fields, half, members, 2 * nx // cols), jnp.float32
        ),
        compiler_params=pltpu.CompilerParams(vmem_limit_bytes=48 * 1024 * 1024),
        name="forecast",
    )(x)


def unshuffle_kernel(x_ref, o_ref):
    cols, _, half, slots, lanes = x_ref.shape
    width = lanes // 2
    low = lax.broadcasted_iota(jnp.int32, (slots, lanes), 1) < width
    for q in range(half):
        for p in range(cols // 2):
            first = x_ref[2 * p, 0, q]
            second = x_ref[2 * p + 1, 0, q]
            top = jnp.where(low, first, pltpu.roll(second, width, 1))
            bottom = jnp.where(low, pltpu.roll(first, width, 1), second)
            o_ref[0, :, q, p * lanes : (p + 1) * lanes] = top
            o_ref[0, :, half + q, p * lanes : (p + 1) * lanes] = bottom


def unshuffle(x):
    cols, fields, half, slots, lanes = x.shape
    nx = cols * lanes // 2
    return pl.pallas_call(
        unshuffle_kernel,
        grid=(fields,),
        in_specs=[pl.BlockSpec((cols, 1, half, slots, lanes), lambda f: (0, f, 0, 0, 0))],
        out_specs=pl.BlockSpec((1, slots, 2 * half, nx), lambda f: (f, 0, 0, 0)),
        out_shape=jax.ShapeDtypeStruct((fields, slots, 2 * half, nx), jnp.float32),
        compiler_params=pltpu.CompilerParams(vmem_limit_bytes=32 * 1024 * 1024),
        name="unshuffle",
    )(x)


def dot(a, b):
    return jnp.dot(a, b, precision=HIGHEST, preferred_element_type=jnp.float32)


def inverse_kernel(g_ref, a_ref, d_ref):
    size = g_ref.shape[0]
    a_ref[...] = g_ref[...]
    row_id = lax.broadcasted_iota(jnp.int32, (BLOCK, BLOCK), 0)
    lane_id = lax.broadcasted_iota(jnp.int32, (BLOCK, BLOCK), 1)
    lane_row = lax.broadcasted_iota(jnp.int32, (1, BLOCK), 1)

    def block_step(b, carry):
        at = pl.ds(pl.multiple_of(b * BLOCK, BLOCK), BLOCK)
        d_ref[...] = a_ref[at, at]

        def outer(o, c):
            base = pl.multiple_of(o * 8, 8)
            for i in range(8):
                k = base + i
                a = d_ref[...]
                row = d_ref[pl.ds(k, 1), :]
                col = jnp.sum(jnp.where(lane_id == k, a, 0.0), axis=1, keepdims=True)
                pivot = jnp.sum(jnp.where(lane_row == k, row, 0.0), axis=1, keepdims=True)
                inv = 1.0 / pivot
                scaled = jnp.where(lane_row == k, inv, row * inv)
                kept = jnp.where(lane_id == k, 0.0, a)
                d_ref[...] = jnp.where(row_id == k, scaled, kept - col * scaled)
            return c

        lax.fori_loop(0, BLOCK // 8, outer, 0)
        inv = d_ref[...]
        inv = 0.5 * (inv + inv.T)
        side = a_ref[:, at]
        row = dot(inv, a_ref[at, :])
        back = -dot(side, inv)
        a_ref[...] = a_ref[...] - dot(side, row)
        a_ref[:, at] = back
        a_ref[at, :] = row
        a_ref[at, at] = inv
        return carry

    lax.fori_loop(0, size // BLOCK, block_step, 0)


def inverse(gram):
    size = gram.shape[0]
    return pl.pallas_call(
        inverse_kernel,
        out_shape=jax.ShapeDtypeStruct((size, size), jnp.float32),
        scratch_shapes=[pltpu.VMEM((BLOCK, BLOCK), jnp.float32)],
        cost_estimate=pl.CostEstimate(
            flops=200 * size**3, bytes_accessed=8 * size * size, transcendentals=0
        ),
        compiler_params=pltpu.CompilerParams(vmem_limit_bytes=32 * 1024 * 1024),
        name="inverse",
    )(gram)


def shifted(x, axis):
    count = lax.axis_size(axis)
    up = lax.ppermute(x, axis, [(i, (i + 1) % count) for i in range(count)])
    down = lax.ppermute(x, axis, [((i + 1) % count, i) for i in range(count)])
    return up, down


def nearby(x):
    slots, obs = x.shape
    tall = jnp.concatenate([x, *shifted(x, "space")], axis=1)
    return jnp.concatenate([tall, *shifted(tall, "members")], axis=1)


def local(ensemble, obs_cells, obs_values, obs_var, obs_noise, assign):
    space = lax.axis_size("space")
    cols = lax.axis_size("members")
    fields, here, rows, nx = ensemble.shape
    width = nx // cols
    half = rows // 2
    lanes = 2 * width
    each = here // space

    split = jnp.transpose(ensemble.reshape(fields, space, each, rows, nx), (1, 0, 2, 3, 4))
    whole = lax.all_to_all(split, "space", 0, 0, tiled=True)
    tiles = forecast(whole, cols)
    tiles = tiles.reshape(cols * space, fields * half, each, lanes)
    tiles = lax.all_to_all(tiles, ("members", "space"), 0, 0, tiled=True)
    count = cols * space * each
    tile = jnp.transpose(tiles, (1, 0, 2, 3)).reshape(fields * half, count, lanes)

    cells = obs_cells.reshape(-1)
    field_of = cells // (rows * width)
    row_of = cells // width % rows
    group_of = field_of * half + row_of % half
    lane_of = row_of // half * width + cells % width
    shape = (fields * half, lanes, cells.shape[0])
    pick = (
        (lax.broadcasted_iota(jnp.int32, shape, 0) == group_of[None, None, :])
        & (lax.broadcasted_iota(jnp.int32, shape, 1) == lane_of[None, None, :])
    ).astype(jnp.float32)
    observed = jnp.einsum("gmc,gco->mo", tile, pick, precision=HIGHEST)
    scale = 1.0 / jnp.sqrt(obs_var.reshape(-1))
    mean_obs = jnp.mean(observed, axis=0, keepdims=True)
    spread = (observed - mean_obs) * scale
    noise = jnp.take(obs_noise.reshape(count, -1), assign, axis=0)
    misfit = (obs_values.reshape(-1)[None, :] - observed) * scale + noise

    near = nearby(spread)
    near_misfit = nearby(misfit)
    gram = dot(near, near.T) / (count - 1) + jnp.eye(count, dtype=jnp.float32)
    solved = inverse(gram)
    cross = dot(near_misfit, near.T) / (count - 1)
    mixing = dot(cross, solved)
    anomaly = tile - jnp.mean(tile, axis=1, keepdims=True)
    updated = tile + jnp.einsum("ij,gjc->gic", mixing, anomaly, precision=HIGHEST)

    back = jnp.transpose(updated.reshape(fields * half, cols, here, lanes), (1, 0, 2, 3))
    back = lax.all_to_all(back, "members", 0, 0, tiled=True)
    return unshuffle(back.reshape(cols, fields, half, here, lanes))


def solution(mesh):
    in_specs = (
        P(None, "members", "space", None),
        P("space", "members", None),
        P("space", "members", None),
        P("space", "members", None),
        P(None, "space", "members", None),
        P(),
    )
    out_specs = P(None, "members", "space", None)
    return jax.shard_map(local, mesh=mesh, in_specs=in_specs, out_specs=out_specs, check_vma=False)
```

time: 619 us -> 350 us (0.57); the launches traced: 611 us -> 350 us
  other arithmetic: 173 us -> 0.52 us
  waiting for transfers between devices: 232 us -> 115 us
  Pallas kernels: 0 us -> 81.4 us
  blocking collectives: 40.7 us -> 117 us
  local copies, waits for them, and re-layouts: 82.7 us -> 6.64 us
  starting transfers between devices: 46.8 us -> 10.7 us
  matrix products: 31.9 us -> 18.5 us
    ppermute x20 -> x8, waiting for transfers between devices: 199 us -> 45.6 us  [the longest x4 25.8 us: shifted(): up = lax.ppermute(x, axis, [(i, (i + 1) % count) for i in range(count)])]
    another operation x38 -> x0, other arithmetic: 140 us -> none  [the longest x15 79.6 us: analyse_tile(): factor = jnp.linalg.cholesky(gram)]
    pallas_call x0 -> x3, Pallas kernels: none -> 81.4 us  [the longest x1 57 us: inverse(): pl.pallas_call(inverse_kernel, out_shape=jax.ShapeDtypeStruct((size, size...]
    all_to_all x1 -> x2, blocking collectives: 40.7 us -> 117 us  [the longest x1 77.9 us: local(): whole = lax.all_to_all(split, 'space', 0, 0, tiled=True)]
    ppermute x20 -> x8, starting transfers between devices: 43 us -> 7.06 us  [the longest x4 4.85 us: shifted(): down = lax.ppermute(x, axis, [((i + 1) % count, i) for i in range(count)])]
    all_to_all x1, waiting for transfers between devices: 33.3 us -> 69 us  [local(): tiles = lax.all_to_all(tiles, ('members', 'space'), 0, 0, tiled=True)]
    another operation x21 -> x0, local copies, waits for them, and re-layouts: 19.6 us -> none
    unnamed x43 -> x18, local copies, waits for them, and re-layouts: 18.1 us -> 0.21 us
  transfers between devices with their start and end apart: 21 -> 9, of which waited for: 20 -> 5; matrix products, arithmetic and copies ran while one was open for 1% -> 2% of each run, Pallas kernels for 0% -> 0%
where the time goes in v1:
time: 350 us
  blocking collectives  117 us (33%)
  waiting for transfers between devices  115 us (33%)
  Pallas kernels  81.4 us (23%)
  matrix products  18.5 us (5%)
  starting transfers between devices  10.7 us (3%)
  local copies, waits for them, and re-layouts  6.64 us (2%)
    all_to_all x1, blocking collectives, local(): whole = lax.all_to_all(split, 'space', 0, 0, tiled=True)  77.9 us
    all_to_all x1, waiting for transfers between devices, local(): tiles = lax.all_to_all(tiles, ('members', 'space'), 0, 0, tiled=True)  69 us
    pallas_call x1, Pallas kernels, inverse(): pl.pallas_call(inverse_kernel, out_shape=jax.ShapeDtypeStruct((size, size...  57 us
    all_to_all x1, blocking collectives, local(): back = lax.all_to_all(back, 'members', 0, 0, tiled=True)  39.4 us
    ppermute x4, waiting for transfers between devices, shifted(): up = lax.ppermute(x, axis, [(i, (i + 1) % count) for i in range(count)])  25.8 us
    pallas_call x1, Pallas kernels, forecast(): pl.pallas_call(functools.partial(forecast_kernel, cols, half), grid=(memb...  20.8 us
    ppermute x4, waiting for transfers between devices, shifted(): down = lax.ppermute(x, axis, [((i + 1) % count, i) for i in range(count)])  19.7 us
    dot_general x3, matrix products, dot(): return jnp.dot(a, b, precision=HIGHEST, preferred_element_type=jnp.float32)  10.7 us
  transfers between devices with their start and end apart: 9, of which 5 were waited for; matrix products, arithmetic and copies ran while one was open for 2% of the time, Pallas kernels for 0%

profile of v1, /device:TPU:0, one launch (start us, length us, event | category | flops | bytes accessed | tf_op | source)
XLA Modules:
  0.0 349.9 jit_solution(6811897822195784788)
XLA Ops:
  0.0 0.0 copy-start
  0.0 2.2 copy.23
  2.3 77.9 %all_to_all.15.x_ref = f32[8,3,16,8,256]{4,3,2,1,0:T(8,128)} all-to-all(f32[8,3,16,8,256]{4,3,2,1,0:T(8,128)S(1)} %bitcast.47), channel_id=1, replica_groups=mesh['members'=4,'space'=8] {'space'}, dimensions={0} | all-to-all | bytes 6291456 | tf_op jit(solution)/shard_map/all_to_all | solution.py:204
  80.1 20.8 %forecast.1 = f32[4,8,3,4,16,128]{5,4,3,2,1,0:T(8,128)} custom-call(f32[8,3,16,8,256]{4,3,2,1,0:T(8,128)} %all_to_all.15.x_ref), custom_call_target="tpu_custom_call" | custom-call | tf_op jit(solution)/shard_map/forecast/pallas_call | solution.py:80
  101.0 0.0 copy-start.2
  101.0 3.6 %all-to-all-start.1 = ((f32[32,12,16,128]{3,2,1,0:T(8,128)}), f32[32,12,16,128]{3,2,1,0:T(8,128)S(1)}, u32[]{:S(2)}, u32[]{:S(2)}) async-start(f32[32,12,16,128]{3,2,1,0:T(8,128)} %bitcast.2), calls=%async_computation.1 | async-start | bytes 6291456 | tf_op jit(solution)/shard_map/all_to_all | solution.py:207
  104.6 0.0 copy-done.2
  104.6 0.0 copy-start.4
  104.6 0.0 copy-start.5
  104.7 0.0 copy-done
  104.7 1.6 gather_fusion
  106.3 1.8 copy.14
  108.1 0.0 copy-done.4
  108.1 0.0 copy-done.5
  108.2 69.0 %all-to-all-done.1 = f32[32,12,16,128]{3,2,1,0:T(8,128)S(1)} async-done(((f32[32,12,16,128]{3,2,1,0:T(8,128)}), f32[32,12,16,128]{3,2,1,0:T(8,128)S(1)}, u32[]{:S(2)}, u32[]{:S(2)}) %all-to-all-start.1) | async-done | bytes 3145760 | tf_op jit(solution)/shard_map/all_to_all | solution.py:207
  177.1 0.3 copy.13
  177.5 0.0 copy-start.1
  177.5 0.0 copy-start.3
  177.5 2.0 fusion.15
  179.5 0.0 copy-done.1
  179.5 0.0 copy-done.3
  179.5 0.2 constant_dynamic-update-slice_fusion.9
  179.7 0.1 collective-permute-start.1
  179.7 2.0 collective-permute-start
  181.7 2.8 collective-permute-start.5
  184.5 0.0 collective-permute-start.4
  184.5 0.2 bitcast_reduce_fusion
  184.7 15.4 %collective-permute-done.1 = f32[512,128]{0,1:T(8,128)S(1)} collective-permute-done((f32[512,128]{0,1:T(8,128)S(1)}, f32[512,128]{0,1:T(8,128)S(1)}, u32[]{:S(2)}, u32[]{:S(2)}) %collective-permute-start.1) | collective-permute-done | bytes 262176 | tf_op jit(solution)/shard_map/ppermute | solution.py:184
  200.1 0.0 collective-permute-done
  200.1 0.1 pad_maximum_fusion
  200.2 0.1 collective-permute-start.2
  200.2 4.3 %collective-permute-done.5 = f32[512,128]{0,1:T(8,128)S(1)} collective-permute-done((f32[512,128]{0,1:T(8,128)S(1)}, f32[512,128]{0,1:T(8,128)S(1)}, u32[]{:S(2)}, u32[]{:S(2)}) %collective-permute-start.5) | collective-permute-done | bytes 262176 | tf_op jit(solution)/shard_map/ppermute | solution.py:184
  204.5 0.0 collective-permute-done.4
  204.5 0.1 pad_maximum_fusion.1
  204.6 0.4 collective-permute-start.7
  205.0 0.1 collective-permute-start.6
  205.2 1.6 collective-permute-start.3
  206.9 9.0 %collective-permute-done.2 = f32[512,384]{0,1:T(8,128)S(1)} collective-permute-done((f32[512,384]{0,1:T(8,128)S(1)}, f32[512,384]{0,1:T(8,128)S(1)}, u32[]{:S(2)}, u32[]{:S(2)}) %collective-permute-start.2) | collective-permute-done | bytes 786464 | tf_op jit(solution)/shard_map/ppermute | solution.py:183
  215.9 0.1 constant_dynamic-update-slice_fusion.1
  216.0 16.8 %collective-permute-done.6 = f32[512,384]{0,1:T(8,128)S(1)} collective-permute-done((f32[512,384]{0,1:T(8,128)S(1)}, f32[512,384]{0,1:T(8,128)S(1)}, u32[]{:S(2)}, u32[]{:S(2)}) %collective-permute-start.6) | collective-permute-done | bytes 786464 | tf_op jit(solution)/shard_map/ppermute | solution.py:183
  232.8 0.1 constant_dynamic-update-slice_fusion.6
  232.8 0.0 collective-permute-done.7
  232.8 0.1 constant_dynamic-update-slice_fusion.5
  232.9 4.4 %fusion.5.g_ref = f32[512,512]{1,0:T(8,128)S(1)} fusion(f32[512,1152]{0,1:T(8,128)S(1)} %constant_dynamic-update-slice_fusion.5), kind=kOutput, calls=%fused_computation.9 | convolution fusion | flops 3624927232 | bytes 3407872 | tf_op jit(solution)/shard_map/dot_general | solution.py:124
  237.3 0.0 collective-permute-done.3
  237.4 0.1 constant_dynamic-update-slice_fusion
  237.4 4.4 %convolution_multiply_fusion.1 = f32[512,512]{1,0:T(8,128)S(1)} fusion(f32[512,1152]{0,1:T(8,128)S(1)} %constant_dynamic-update-slice_fusion, f32[512,1152]{0,1:T(8,128)S(1)} %constant_dynamic-update-slice_fusion.5), kind=kOutput, calls=%fused_computation.10 | convolution fusion | flops 3624140800 | bytes 5767168 | tf_op jit(solution)/shard_map/dot_general | solution.py:124
  241.8 57.0 %inverse.1 = f32[512,512]{1,0:T(8,128)S(1)} custom-call(f32[512,512]{1,0:T(8,128)S(1)} %fusion.5.g_ref), custom_call_target="tpu_custom_call" | custom-call | flops 26843545600 | bytes 2097152 | tf_op jit(solution)/shard_map/inverse/pallas_call | solution.py:169
  298.9 1.8 convolution_bitcast_fusion
  300.7 5.8 %bitcast_add_fusion = f32[12,512,128]{2,1,0:T(8,128)S(1)} fusion(f32[12,512,128]{2,1,0:T(8,128)S(1)} %bitcast.45, f32[512,512,1]{1,0,2:T(8,128)S(1)} %convolution_bitcast_fusion, f32[12,128]{1,0:T(8,128)S(1)} %broadcast_multiply_fusion), kind=kOutput, calls=%fused_computation.1 | convolution fusion | flops 4833411072 | bytes 7346176 | tf_op jit(solution)/shard_map/ij,gjc->gic/dot_general | solution.py:235
  306.5 0.3 copy.22
  306.8 39.4 %all_to_all.16 = f32[4,12,128,128]{3,2,1,0:T(8,128)S(1)} all-to-all(f32[4,12,128,128]{3,2,1,0:T(8,128)S(1)} %bitcast.46), channel_id=1, replica_groups=mesh['members'=4,'space'=8] {'members'}, dimensions={0} | all-to-all | bytes 6291456 | tf_op jit(solution)/shard_map/all_to_all | solution.py:238
  346.3 3.6 %unshuffle.1 = f32[3,128,8,256]{3,2,1,0:T(8,128)} custom-call(f32[4,3,4,128,128]{4,3,2,1,0:T(8,128)S(1)} %bitcast.42), custom_call_target="tpu_custom_call" | custom-call | tf_op jit(solution)/shard_map/unshuffle/pallas_call | solution.py:112
  (12 shorter events, 0.1 us)
Async XLA Ops:
  0.0 104.7 %copy-start = (f32[512,1,1,128]{3,2,1,0:T(1,128)S(1)}, f32[512,1,1,128]{3,2,1,0:T(1,128)}, u32[]{:S(2)}) copy-start(f32[512,1,1,128]{3,2,1,0:T(1,128)} %param.10) | copy-start | bytes 786436
  101.0 3.6 %copy-start.2 = (s32[512]{0:T(512)S(1)}, s32[512]{0:T(512)}, u32[]{:S(2)}) copy-start(s32[512]{0:T(512)} %param.11) | copy-start | bytes 6148
  101.0 76.2 %all-to-all-start.1 = ((f32[32,12,16,128]{3,2,1,0:T(8,128)}), f32[32,12,16,128]{3,2,1,0:T(8,128)S(1)}, u32[]{:S(2)}, u32[]{:S(2)}) async-start(f32[32,12,16,128]{3,2,1,0:T(8,128)} %bitcast.2), calls=%async_computation.1 | async-start | bytes 6291456 | tf_op jit(solution)/shard_map/all_to_all | solution.py:207
  104.6 3.5 copy-start.4
  104.6 3.5 copy-start.5
  177.5 2.0 copy-start.1
  177.5 2.0 copy-start.3
  179.7 20.5 %collective-permute-start.1 = (f32[512,128]{0,1:T(8,128)S(1)}, f32[512,128]{0,1:T(8,128)S(1)}, u32[]{:S(2)}, u32[]{:S(2)}) collective-permute-start(f32[512,128]{0,1:T(8,128)S(1)} %get-tuple-element.12), channel_id=1, source_target_pairs={{1,0},{2,1},{3,2},{4,3},{5,4},{6,5},{7,6},{0,7},{9,8},{10,9},{11,1... | collective-permute-start | bytes 786440 | tf_op jit(solution)/shard_map/ppermute | solution.py:184
  179.7 20.4 %collective-permute-start = (f32[512,128]{0,1:T(8,128)S(1)}, f32[512,128]{0,1:T(8,128)S(1)}, u32[]{:S(2)}, u32[]{:S(2)}) collective-permute-start(f32[512,128]{0,1:T(8,128)S(1)} %get-tuple-element.12), channel_id=1, source_target_pairs={{0,1},{1,2},{2,3},{3,4},{4,5},{5,6},{6,7},{7,0},{8,9},{9,10},{10,1... | collective-permute-start | bytes 786440 | tf_op jit(solution)/shard_map/ppermute | solution.py:183
  181.7 22.8 %collective-permute-start.5 = (f32[512,128]{0,1:T(8,128)S(1)}, f32[512,128]{0,1:T(8,128)S(1)}, u32[]{:S(2)}, u32[]{:S(2)}) collective-permute-start(f32[512,128]{0,1:T(8,128)S(1)} %get-tuple-element.6), channel_id=1, source_target_pairs={{1,0},{2,1},{3,2},{4,3},{5,4},{6,5},{7,6},{0,7},{9,8},{10,9},{11,1... | collective-permute-start | bytes 786440 | tf_op jit(solution)/shard_map/ppermute | solution.py:184
  184.5 20.0 %collective-permute-start.4 = (f32[512,128]{0,1:T(8,128)S(1)}, f32[512,128]{0,1:T(8,128)S(1)}, u32[]{:S(2)}, u32[]{:S(2)}) collective-permute-start(f32[512,128]{0,1:T(8,128)S(1)} %get-tuple-element.6), channel_id=1, source_target_pairs={{0,1},{1,2},{2,3},{3,4},{4,5},{5,6},{6,7},{7,0},{8,9},{9,10},{10,1... | collective-permute-start | bytes 786440 | tf_op jit(solution)/shard_map/ppermute | solution.py:183
  200.2 15.7 %collective-permute-start.2 = (f32[512,384]{0,1:T(8,128)S(1)}, f32[512,384]{0,1:T(8,128)S(1)}, u32[]{:S(2)}, u32[]{:S(2)}) collective-permute-start(f32[512,384]{0,1:T(8,128)S(1)} %pad_maximum_fusion), channel_id=1, source_target_pairs={{0,8},{8,16},{16,24},{24,0},{1,9},{9,17},{17,25},{25,1},{2,10},{10... | collective-permute-start | bytes 2359304 | tf_op jit(solution)/shard_map/ppermute | solution.py:183
  204.6 28.2 %collective-permute-start.7 = (f32[512,384]{0,1:T(8,128)S(1)}, f32[512,384]{0,1:T(8,128)S(1)}, u32[]{:S(2)}, u32[]{:S(2)}) collective-permute-start(f32[512,384]{0,1:T(8,128)S(1)} %pad_maximum_fusion.1), channel_id=1, source_target_pairs={{8,0},{16,8},{24,16},{0,24},{9,1},{17,9},{25,17},{1,25},{10,2},{18... | collective-permute-start | bytes 2359304 | tf_op jit(solution)/shard_map/ppermute | solution.py:184
  205.0 27.8 %collective-permute-start.6 = (f32[512,384]{0,1:T(8,128)S(1)}, f32[512,384]{0,1:T(8,128)S(1)}, u32[]{:S(2)}, u32[]{:S(2)}) collective-permute-start(f32[512,384]{0,1:T(8,128)S(1)} %pad_maximum_fusion.1), channel_id=1, source_target_pairs={{0,8},{8,16},{16,24},{24,0},{1,9},{9,17},{17,25},{25,1},{2,10},{10... | collective-permute-start | bytes 2359304 | tf_op jit(solution)/shard_map/ppermute | solution.py:183
  205.2 32.2 %collective-permute-start.3 = (f32[512,384]{0,1:T(8,128)S(1)}, f32[512,384]{0,1:T(8,128)S(1)}, u32[]{:S(2)}, u32[]{:S(2)}) collective-permute-start(f32[512,384]{0,1:T(8,128)S(1)} %pad_maximum_fusion), channel_id=1, source_target_pairs={{8,0},{16,8},{24,16},{0,24},{9,1},{17,9},{25,17},{1,25},{10,2},{18... | collective-permute-start | bytes 2359304 | tf_op jit(solution)/shard_map/ppermute | solution.py:184
